TPU v7x, 128 devices: a whole 4x4x4 slice. The times are simulated.
128 devices in a mesh: group: 8 (over y, x_hi), strip: 16 (over x_lo, z, core).
Axes of the slice: x: 4 (x_hi: 2, x_lo: 2; x = x_hi * 2 + x_lo), y: 4, z: 4, core: 2. Of those that a mesh axis runs over, the one named last changes fastest.
Arguments:
- initial: float32 [8, 512, 1024], P('group', 'strip'), may hold values from -6 to 6
- conductivity: float32 [8, 512, 1024], P('group', 'strip'), may hold values from 0.5 to 1.5
- step_count: int32 [8], P('group'), may hold values from 16 to 32, as said below
- emit_steps: int32 [8, 16], P('group'), may hold values from 1 to 32
- assign: int32 [512], replicated, may hold values from 0 to 127
- sample_inputs: bfloat16 [512, 128], P(('group', 'strip')), may hold values from -6 to 6
- w_first: bfloat16 [128, 512], replicated, may hold values from -0.5 to 0.5
- w_second: bfloat16 [512, 512], replicated, may hold values from -0.25 to 0.25
- w_third: bfloat16 [512, 512], replicated, may hold values from -0.25 to 0.25
- w_out: bfloat16 [512, 512, 1024], P(None, 'strip', 'group'), may hold values from -0.25 to 0.25
Outputs:
- grad_first: float32 [128, 512], replicated
- grad_second: float32 [512, 512], replicated
- grad_third: float32 [512, 512], replicated
- grad_out: bfloat16 [512, 512, 1024], P(None, 'strip', 'group')
Inputs may be any that keep to these rules, and one draw needn't show every extreme that they name: `step_count`: at least 16; some field runs all 32 steps.
All inputs are finite; a program needn't handle non-finite values.
Results may differ from a plain program's by a relative error of at most 0.0039.
The roundings to bfloat16 on the way count: a program that leaves them out, or rounds other values in their place, can miss the bound.
Values may be sent and summed in bfloat16 or wider, within the bound.
A program may use at most 64 MiB of HBM per device.

v0:
```python
import jax
import jax.numpy as jnp
from jax import lax
from jax.sharding import PartitionSpec as P

STEPS = 32
step_rate = 0.125


def padded(x, sides, width):
    for axis, dim in sides:
        count, length = (lax.axis_size(axis), x.shape[dim])
        up = [(i, (i + 1) % count) for i in range(count - 1)]
        down = [(j, i) for i, j in up]
        last = lax.slice_in_dim(x, length - width, length, axis=dim)
        initial = lax.slice_in_dim(x, 0, width, axis=dim)
        before = lax.ppermute(last, axis, up)
        after = lax.ppermute(initial, axis, down)
        x = jnp.concatenate([before, x, after], axis=dim)
    return x


def stencil(current, kappa_rows):
    middle = current[1:-1]
    zero_column = jnp.zeros((middle.shape[0], 1), jnp.float32)
    east_side = jnp.concatenate([middle[:, 1:], zero_column], axis=1)
    west_side = jnp.concatenate([zero_column, middle[:, :-1]], axis=1)
    beside_all = current[2:] + current[:-2] + east_side + west_side
    return middle + step_rate * kappa_rows * (1.0 + 0.25 * jnp.tanh(middle)) * (
        beside_all - 4.0 * middle
    )


def record(history, step_index, inner):
    return lax.dynamic_update_slice_in_dim(history, inner.astype(jnp.bfloat16)[None], step_index, 0)


def contract_rows(left, right):
    return lax.dot_general(
        left, right, (((0,), (0,)), ((), ())), preferred_element_type=jnp.float32
    )


def contract_cols(left, right):
    return lax.dot_general(
        left, right, (((1,), (1,)), ((), ())), preferred_element_type=jnp.float32
    )


def forward(inputs, w_first, w_second, w_third):
    act_a = jnp.tanh(jnp.dot(inputs, w_first, preferred_element_type=jnp.float32))
    hidden_a = act_a.astype(jnp.bfloat16)
    act_b = jnp.tanh(jnp.dot(hidden_a, w_second, preferred_element_type=jnp.float32))
    hidden_b = act_b.astype(jnp.bfloat16)
    act_c = jnp.tanh(jnp.dot(hidden_b, w_third, preferred_element_type=jnp.float32))
    hidden_c = act_c.astype(jnp.bfloat16)
    return ((act_a, act_b, act_c), (hidden_a, hidden_b, hidden_c))


def backward(inputs, activations, hiddens, w_second, w_third, back_c):
    delta_c = (back_c * (1.0 - activations[2] * activations[2])).astype(jnp.bfloat16)
    grad_third = contract_rows(hiddens[1], delta_c)
    back_b = contract_cols(delta_c, w_third)
    delta_b = (back_b * (1.0 - activations[1] * activations[1])).astype(jnp.bfloat16)
    grad_second = contract_rows(hiddens[0], delta_b)
    back_a = contract_cols(delta_b, w_second)
    delta_a = (back_a * (1.0 - activations[0] * activations[0])).astype(jnp.bfloat16)
    grad_first = contract_rows(inputs, delta_a)
    return (grad_first, grad_second, grad_third)


def per_device(
    initial,
    conductivity,
    step_count,
    emit_steps,
    assign,
    sample_inputs,
    w_first,
    w_second,
    w_third,
    w_out,
):
    field_now = initial[0]
    kappa = conductivity[0]
    run_steps = step_count[0]
    emit_row = emit_steps[0]
    row_count = field_now.shape[0]
    start_history = jnp.zeros((STEPS, row_count, field_now.shape[1]), jnp.bfloat16)
    halo_width = 4
    kappa_wide = padded(kappa, (("strip", 0),), halo_width)
    first_row = lax.axis_index("strip") * row_count - halo_width
    global_rows = first_row + jnp.arange(row_count + 2 * halo_width, dtype=jnp.int32)
    inside = ((global_rows >= 0) & (global_rows < row_count * lax.axis_size("strip"))).astype(
        jnp.float32
    )[:, None]

    def block_steps(block_index, carried):
        current, history = carried
        widened = padded(current, (("strip", 0),), halo_width)
        for substep in range(halo_width):
            step_index = block_index * halo_width + substep
            low_row = substep + 1
            span_rows = row_count + 2 * (halo_width - substep - 1)
            candidate = (
                stencil(widened, kappa_wide[low_row : low_row + span_rows])
                * inside[low_row : low_row + span_rows]
            )
            widened = jnp.where(step_index < run_steps, candidate, widened[1:-1])
            offset = halo_width - substep - 1
            history = record(history, step_index, widened[offset : offset + row_count])
        return (widened, history)

    field_now, history = lax.fori_loop(
        0, STEPS // halo_width, block_steps, (field_now, start_history)
    )
    snapshots = jnp.take(history, emit_row - 1, axis=0)
    regrouped = lax.all_to_all(snapshots[None], "group", split_axis=3, concat_axis=0, tiled=True)
    flat_snaps = regrouped.reshape(regrouped.shape[0] * regrouped.shape[1], -1)
    targets = jnp.take(flat_snaps, assign, axis=0)
    weight_flat = w_out.reshape(w_out.shape[0], -1)
    inverse_root = 1.0 / jnp.sqrt(jnp.float32(assign.shape[0]))
    all_inputs = lax.all_gather(sample_inputs, ("group", "strip"), axis=0, tiled=True)
    activations, hiddens = forward(all_inputs, w_first, w_second, w_third)
    hidden_all = hiddens[2]
    predicted = jnp.dot(hidden_all, weight_flat, preferred_element_type=jnp.float32)
    residual = ((predicted - targets.astype(jnp.float32)) * inverse_root).astype(jnp.bfloat16)
    grad_out = contract_rows(hidden_all, residual).astype(jnp.bfloat16)
    residual, grad_out = (residual, grad_out)
    back_c = lax.psum(contract_cols(residual, weight_flat), ("group", "strip"))
    grad_first, grad_second, grad_third = backward(
        all_inputs, activations, hiddens, w_second, w_third, back_c
    )
    return (grad_first, grad_second, grad_third, grad_out.reshape(w_out.shape))


def solution(mesh):
    placed = (
        P("group", "strip", None),
        P("group", "strip", None),
        P("group"),
        P("group", None),
        P(),
        P(("group", "strip"), None),
        P(),
        P(),
        P(),
        P(None, "strip", "group"),
    )
    return jax.shard_map(
        per_device,
        mesh=mesh,
        in_specs=placed,
        out_specs=(P(), P(), P(), P(None, "strip", "group")),
        check_vma=False,
    )
```

profile of v0, /device:TPU:1, one launch (start us, length us, event | category | flops | bytes accessed | tf_op | source)
XLA Modules:
  0.0 374.0 jit_solution(3398122449657235176)
XLA Ops:
  7.2 1.0 copy.49
  8.1 0.8 slice_bitcast_fusion.5
  8.9 4.9 %collective-permute-start.2 = (f32[4,1024]{1,0:T(4,128)S(1)}, f32[4,1024]{1,0:T(4,128)S(1)}, u32[]{:S(2)}, u32[]{:S(2)}) collective-permute-start(f32[4,1024]{1,0:T(4,128)S(1)} %get-tuple-element.221), channel_id=1, source_target_pairs={{0,1},{1,2},{2,3},{3,4},{4,5},{5,6},{6,7},{7,8},{8,9},{9,10},{10,1... | collective-permute-start | bytes 49160 | tf_op jit(solution)/shard_map/ppermute | solution.py:17
  13.8 1.9 collective-permute-start.3
  15.8 0.7 fusion.55
  16.4 0.7 compare_and_fusion
  17.1 0.7 compare_select_fusion
  17.8 0.7 compare_and_fusion.1
  18.5 0.4 collective-permute-done.3
  18.9 0.9 pad_maximum_fusion.1
  19.8 0.3 broadcast_in_dim.69
  20.1 78.7 %while.17 = (s32[]{:T(128)}, f32[32,1024]{1,0:T(8,128)S(1)}, bf16[32,32,1024]{2,1,0:T(8,128)(2,1)S(1)}, s32[]{:T(128)}, f32[40,1024]{1,0:T(8,128)S(1)}, /*index=...) while((s32[]{:T(128)}, f32[32,1024]{1,0:T(8,128)S(1)}, ...), condition=%wide.region_1.2_spmd, body=%wide.region_0.1_spmd.sunk | while | flops 1978390 | bytes 7814625 | solution.py:114
  20.1 2.1 collective-permute-start
  22.2 3.6 collective-permute-start.1
  28.9 0.1 fusion.89
  29.2 0.1 fusion.92
  30.0 2.1 collective-permute-start
  32.0 3.6 collective-permute-start.1
  38.8 0.1 fusion.89
  39.0 0.1 fusion.92
  39.8 2.1 collective-permute-start
  41.9 3.6 collective-permute-start.1
  48.6 0.1 fusion.89
  48.9 0.1 fusion.92
  49.7 2.1 collective-permute-start
  51.7 3.6 collective-permute-start.1
  58.4 0.1 fusion.89
  58.7 0.1 fusion.92
  59.5 2.1 collective-permute-start
  61.6 3.6 collective-permute-start.1
  68.3 0.1 fusion.89
  68.5 0.1 fusion.92
  69.3 2.1 collective-permute-start
  71.4 3.6 collective-permute-start.1
  79.2 2.1 collective-permute-start
  81.2 3.6 collective-permute-start.1
  89.0 2.1 collective-permute-start
  91.1 3.6 collective-permute-start.1
  98.8 1.6 gather_fusion
  100.4 1.4 bitcast_select_fusion
  101.8 4.7 %copy.18 = bf16[1,16,32,1024]{2,1,0,3:T(8,128)(2,1)} copy(bf16[1,16,32,1024]{3,2,1,0:T(8,128)(2,1)S(1)} %bitcast_select_fusion) | data formatting | bytes 2097152 | tf_op jit(solution)/shard_map/jit(_take)/select_n | solution.py:117
  106.5 7.9 %reshape.112 = bf16[8,2,32768]{2,1,0:T(2,128)(2,1)} reshape(bf16[1024,1,16,32]{3,2,1,0:T(8,128)(2,1)} %bitcast.94) | data formatting | bytes 2097152
  114.4 6.7 %all-to-all-start = ((bf16[8,2,32768]{2,1,0:T(2,128)(2,1)}), bf16[8,2,32768]{2,1,0:T(2,128)(2,1)S(1)}, u32[]{:S(2)}, u32[]{:S(2)}) async-start(bf16[8,2,32768]{2,1,0:T(2,128)(2,1)} %reshape.112), calls=%async_computation | async-start | bytes 2097152 | tf_op jit(solution)/shard_map/all_to_all | solution.py:118
  121.1 57.0 %all-gather = bf16[128,4,128]{2,1,0:T(4,128)(2,1)S(1)} all-gather(bf16[1,4,128]{2,1,0:T(4,128)(2,1)S(1)} %bitcast.103), channel_id=1, replica_groups=mesh['group'=8,'strip'=16] {'group','strip'}, dimensions={0}, use_global_device_ids=true | all-gather | bytes 132096 | tf_op jit(solution)/shard_map/all_gather | solution.py:123
  178.2 0.3 convolution_tanh_fusion.2
  178.5 0.4 convolution_tanh_fusion.1
  178.9 1.0 copy-done.1
  179.9 1.4 convolution_tanh_fusion
  181.3 4.5 %reshape.113 = bf16[1024,1,16,32]{3,2,1,0:T(8,128)(2,1)} reshape(bf16[8,2,32768]{2,1,0:T(2,128)(2,1)S(1)} %all-to-all-done) | data formatting | bytes 2097152
  185.8 5.5 %copy.19 = bf16[1,16,32,8,128]{4,2,1,3,0:T(8,128)(2,1)} copy(bf16[1,16,32,8,128]{2,1,4,3,0:T(8,128)(2,1)} %bitcast.95) | data formatting | bytes 2097152 | tf_op jit(solution)/shard_map/all_to_all | solution.py:118
  191.3 1.7 copy.33
  193.0 4.4 %gather_fusion.1 = bf16[512,4096]{1,0:T(8,128)(2,1)} fusion(bf16[128,4096]{1,0:T(8,128)(2,1)S(1)} %bitcast.93, s32[1024]{0:T(1024)S(1)} %pad_clamp_fusion), kind=kCustom, calls=%fused_computation.1 | custom fusion | bytes 8390656 | tf_op jit(solution)/shard_map/jit(_take)/gather | solution.py:120
  197.4 6.9 %multiply_convert_fusion = bf16[512,4096]{1,0:T(8,128)(2,1)S(1)} fusion(bf16[512,4096]{1,0:T(8,128)(2,1)} %gather_fusion.1, pred[512]{0:T(512)(128)(4,1)S(1)} %compare_and_fusion.1, bf16[64,8,32,128]{3,2,1,0:T(8,128)(2,1)} %bitcast.104, f32[512,512]{1,0:T(8,128)} %convolution_tanh_fusion), kind=kOutput, calls=%fused_computation.49 | convolution fusion | flops 2158231552 | bytes 13632000 | tf_op jit(solution)/shard_map/dot_general | solution.py:126
  204.3 2.0 copy-done.5
  206.3 3.9 %fusion.34 = f32[512,512]{1,0:T(8,128)} fusion(bf16[512,4096]{1,0:T(8,128)(2,1)S(1)} %multiply_convert_fusion, bf16[64,8,32,128]{3,2,1,0:T(8,128)(2,1)S(1)} %bitcast.105), kind=kOutput, calls=%fused_computation.51 | convolution fusion | flops 2147483648 | bytes 9437184 | tf_op jit(solution)/shard_map/dot_general | solution.py:45
  210.2 4.6 %fusion.39 = bf16[64,8,32,128]{3,1,2,0:T(8,128)(2,1)S(1)} fusion(bf16[512,4096]{1,0:T(8,128)(2,1)} %copy-done.5, f32[512,512]{1,0:T(8,128)S(1)} %copy-done.3), kind=kOutput, calls=%fused_computation.56 | convolution fusion | flops 2149842944 | bytes 9437184 | tf_op jit(solution)/shard_map/dot_general | solution.py:39
  214.8 3.3 copy.23
  218.1 139.1 %all-reduce.10.cloned.1.call-done = f32[512,512]{1,0:T(8,128)} async-done(((f32[512,512]{1,0:T(8,128)}), f32[512,512]{1,0:T(8,128)}) %all-reduce.10.cloned.1.call-update) | async-done | bytes 1048592 | tf_op jit(solution)/shard_map/psum | solution.py:130
  357.2 1.8 multiply_convert_fusion.1
  359.0 1.3 fusion.40
  360.3 2.1 fusion.43
  362.4 2.5 fusion.52
  364.8 1.4 fusion.49
  366.3 0.8 copy.20
  (181 shorter events, 9.7 us)
Async XLA Ops:
  7.2 172.8 %copy-start = (bf16[512,512]{1,0:T(8,128)(2,1)S(1)}, bf16[512,512]{1,0:T(8,128)(2,1)}, u32[]{:S(2)}) copy-start(bf16[512,512]{1,0:T(8,128)(2,1)} %param.20) | copy-start | bytes 1572868
  8.9 9.6 %collective-permute-start.2 = (f32[4,1024]{1,0:T(4,128)S(1)}, f32[4,1024]{1,0:T(4,128)S(1)}, u32[]{:S(2)}, u32[]{:S(2)}) collective-permute-start(f32[4,1024]{1,0:T(4,128)S(1)} %get-tuple-element.221), channel_id=1, source_target_pairs={{0,1},{1,2},{2,3},{3,4},{4,5},{5,6},{6,7},{7,8},{8,9},{9,10},{10,1... | collective-permute-start | bytes 49160 | tf_op jit(solution)/shard_map/ppermute | solution.py:17
  13.8 5.1 %collective-permute-start.3 = (f32[4,1024]{1,0:T(4,128)S(1)}, f32[4,1024]{1,0:T(4,128)S(1)}, u32[]{:S(2)}, u32[]{:S(2)}) collective-permute-start(f32[4,1024]{1,0:T(4,128)S(1)} %get-tuple-element.222), channel_id=1, source_target_pairs={{1,0},{2,1},{3,2},{4,3},{5,4},{6,5},{7,6},{8,7},{9,8},{10,9},{11,1... | collective-permute-start | bytes 49160 | tf_op jit(solution)/shard_map/ppermute | solution.py:18
  20.1 9.7 %copy-start.4 = (f32[32,1024]{1,0:T(8,128)S(1)}, f32[32,1024]{1,0:T(8,128)}, u32[]{:S(2)}) copy-start(f32[32,1024]{1,0:T(8,128)} %get-tuple-element.328) | copy-start | bytes 393220 | tf_op jit(solution)/shard_map/while
  20.1 8.6 %collective-permute-start = (f32[4,1024]{1,0:T(4,128)S(1)}, f32[4,1024]{1,0:T(4,128)S(1)}, u32[]{:S(2)}, u32[]{:S(2)}) collective-permute-start(f32[4,1024]{1,0:T(4,128)S(1)} %get-tuple-element.278), channel_id=1, source_target_pairs={{1,0},{2,1},{3,2},{4,3},{5,4},{6,5},{7,6},{8,7},{9,8},{10,9},{11,1... | collective-permute-start | bytes 49160 | tf_op jit(solution)/shard_map/while/body/eval_jaxpr/ppermute | solution.py:18
  22.2 6.6 %collective-permute-start.1 = (f32[4,1024]{1,0:T(4,128)S(1)}, f32[4,1024]{1,0:T(4,128)S(1)}, u32[]{:S(2)}, u32[]{:S(2)}) collective-permute-start(f32[4,1024]{1,0:T(4,128)S(1)} %get-tuple-element.279), channel_id=1, source_target_pairs={{0,1},{1,2},{2,3},{3,4},{4,5},{5,6},{6,7},{7,8},{8,9},{9,10},{10,1... | collective-permute-start | bytes 49160 | tf_op jit(solution)/shard_map/while/body/eval_jaxpr/ppermute | solution.py:17
  29.9 9.7 %copy-start.4 = (f32[32,1024]{1,0:T(8,128)S(1)}, f32[32,1024]{1,0:T(8,128)}, u32[]{:S(2)}) copy-start(f32[32,1024]{1,0:T(8,128)} %get-tuple-element.328) | copy-start | bytes 393220 | tf_op jit(solution)/shard_map/while
  30.0 8.6 %collective-permute-start = (f32[4,1024]{1,0:T(4,128)S(1)}, f32[4,1024]{1,0:T(4,128)S(1)}, u32[]{:S(2)}, u32[]{:S(2)}) collective-permute-start(f32[4,1024]{1,0:T(4,128)S(1)} %get-tuple-element.278), channel_id=1, source_target_pairs={{1,0},{2,1},{3,2},{4,3},{5,4},{6,5},{7,6},{8,7},{9,8},{10,9},{11,1... | collective-permute-start | bytes 49160 | tf_op jit(solution)/shard_map/while/body/eval_jaxpr/ppermute | solution.py:18
  32.0 6.6 %collective-permute-start.1 = (f32[4,1024]{1,0:T(4,128)S(1)}, f32[4,1024]{1,0:T(4,128)S(1)}, u32[]{:S(2)}, u32[]{:S(2)}) collective-permute-start(f32[4,1024]{1,0:T(4,128)S(1)} %get-tuple-element.279), channel_id=1, source_target_pairs={{0,1},{1,2},{2,3},{3,4},{4,5},{5,6},{6,7},{7,8},{8,9},{9,10},{10,1... | collective-permute-start | bytes 49160 | tf_op jit(solution)/shard_map/while/body/eval_jaxpr/ppermute | solution.py:17
  39.8 9.7 %copy-start.4 = (f32[32,1024]{1,0:T(8,128)S(1)}, f32[32,1024]{1,0:T(8,128)}, u32[]{:S(2)}) copy-start(f32[32,1024]{1,0:T(8,128)} %get-tuple-element.328) | copy-start | bytes 393220 | tf_op jit(solution)/shard_map/while
  39.8 8.6 %collective-permute-start = (f32[4,1024]{1,0:T(4,128)S(1)}, f32[4,1024]{1,0:T(4,128)S(1)}, u32[]{:S(2)}, u32[]{:S(2)}) collective-permute-start(f32[4,1024]{1,0:T(4,128)S(1)} %get-tuple-element.278), channel_id=1, source_target_pairs={{1,0},{2,1},{3,2},{4,3},{5,4},{6,5},{7,6},{8,7},{9,8},{10,9},{11,1... | collective-permute-start | bytes 49160 | tf_op jit(solution)/shard_map/while/body/eval_jaxpr/ppermute | solution.py:18
  41.9 6.6 %collective-permute-start.1 = (f32[4,1024]{1,0:T(4,128)S(1)}, f32[4,1024]{1,0:T(4,128)S(1)}, u32[]{:S(2)}, u32[]{:S(2)}) collective-permute-start(f32[4,1024]{1,0:T(4,128)S(1)} %get-tuple-element.279), channel_id=1, source_target_pairs={{0,1},{1,2},{2,3},{3,4},{4,5},{5,6},{6,7},{7,8},{8,9},{9,10},{10,1... | collective-permute-start | bytes 49160 | tf_op jit(solution)/shard_map/while/body/eval_jaxpr/ppermute | solution.py:17
  49.6 9.7 %copy-start.4 = (f32[32,1024]{1,0:T(8,128)S(1)}, f32[32,1024]{1,0:T(8,128)}, u32[]{:S(2)}) copy-start(f32[32,1024]{1,0:T(8,128)} %get-tuple-element.328) | copy-start | bytes 393220 | tf_op jit(solution)/shard_map/while
  49.7 8.6 %collective-permute-start = (f32[4,1024]{1,0:T(4,128)S(1)}, f32[4,1024]{1,0:T(4,128)S(1)}, u32[]{:S(2)}, u32[]{:S(2)}) collective-permute-start(f32[4,1024]{1,0:T(4,128)S(1)} %get-tuple-element.278), channel_id=1, source_target_pairs={{1,0},{2,1},{3,2},{4,3},{5,4},{6,5},{7,6},{8,7},{9,8},{10,9},{11,1... | collective-permute-start | bytes 49160 | tf_op jit(solution)/shard_map/while/body/eval_jaxpr/ppermute | solution.py:18
  51.7 6.6 %collective-permute-start.1 = (f32[4,1024]{1,0:T(4,128)S(1)}, f32[4,1024]{1,0:T(4,128)S(1)}, u32[]{:S(2)}, u32[]{:S(2)}) collective-permute-start(f32[4,1024]{1,0:T(4,128)S(1)} %get-tuple-element.279), channel_id=1, source_target_pairs={{0,1},{1,2},{2,3},{3,4},{4,5},{5,6},{6,7},{7,8},{8,9},{9,10},{10,1... | collective-permute-start | bytes 49160 | tf_op jit(solution)/shard_map/while/body/eval_jaxpr/ppermute | solution.py:17
  59.5 9.7 %copy-start.4 = (f32[32,1024]{1,0:T(8,128)S(1)}, f32[32,1024]{1,0:T(8,128)}, u32[]{:S(2)}) copy-start(f32[32,1024]{1,0:T(8,128)} %get-tuple-element.328) | copy-start | bytes 393220 | tf_op jit(solution)/shard_map/while
  59.5 8.6 %collective-permute-start = (f32[4,1024]{1,0:T(4,128)S(1)}, f32[4,1024]{1,0:T(4,128)S(1)}, u32[]{:S(2)}, u32[]{:S(2)}) collective-permute-start(f32[4,1024]{1,0:T(4,128)S(1)} %get-tuple-element.278), channel_id=1, source_target_pairs={{1,0},{2,1},{3,2},{4,3},{5,4},{6,5},{7,6},{8,7},{9,8},{10,9},{11,1... | collective-permute-start | bytes 49160 | tf_op jit(solution)/shard_map/while/body/eval_jaxpr/ppermute | solution.py:18
  61.6 6.6 %collective-permute-start.1 = (f32[4,1024]{1,0:T(4,128)S(1)}, f32[4,1024]{1,0:T(4,128)S(1)}, u32[]{:S(2)}, u32[]{:S(2)}) collective-permute-start(f32[4,1024]{1,0:T(4,128)S(1)} %get-tuple-element.279), channel_id=1, source_target_pairs={{0,1},{1,2},{2,3},{3,4},{4,5},{5,6},{6,7},{7,8},{8,9},{9,10},{10,1... | collective-permute-start | bytes 49160 | tf_op jit(solution)/shard_map/while/body/eval_jaxpr/ppermute | solution.py:17
  69.3 9.7 %copy-start.4 = (f32[32,1024]{1,0:T(8,128)S(1)}, f32[32,1024]{1,0:T(8,128)}, u32[]{:S(2)}) copy-start(f32[32,1024]{1,0:T(8,128)} %get-tuple-element.328) | copy-start | bytes 393220 | tf_op jit(solution)/shard_map/while
  69.3 8.6 %collective-permute-start = (f32[4,1024]{1,0:T(4,128)S(1)}, f32[4,1024]{1,0:T(4,128)S(1)}, u32[]{:S(2)}, u32[]{:S(2)}) collective-permute-start(f32[4,1024]{1,0:T(4,128)S(1)} %get-tuple-element.278), channel_id=1, source_target_pairs={{1,0},{2,1},{3,2},{4,3},{5,4},{6,5},{7,6},{8,7},{9,8},{10,9},{11,1... | collective-permute-start | bytes 49160 | tf_op jit(solution)/shard_map/while/body/eval_jaxpr/ppermute | solution.py:18
  71.4 6.6 %collective-permute-start.1 = (f32[4,1024]{1,0:T(4,128)S(1)}, f32[4,1024]{1,0:T(4,128)S(1)}, u32[]{:S(2)}, u32[]{:S(2)}) collective-permute-start(f32[4,1024]{1,0:T(4,128)S(1)} %get-tuple-element.279), channel_id=1, source_target_pairs={{0,1},{1,2},{2,3},{3,4},{4,5},{5,6},{6,7},{7,8},{8,9},{9,10},{10,1... | collective-permute-start | bytes 49160 | tf_op jit(solution)/shard_map/while/body/eval_jaxpr/ppermute | solution.py:17
  79.2 9.7 %copy-start.4 = (f32[32,1024]{1,0:T(8,128)S(1)}, f32[32,1024]{1,0:T(8,128)}, u32[]{:S(2)}) copy-start(f32[32,1024]{1,0:T(8,128)} %get-tuple-element.328) | copy-start | bytes 393220 | tf_op jit(solution)/shard_map/while
  79.2 8.6 %collective-permute-start = (f32[4,1024]{1,0:T(4,128)S(1)}, f32[4,1024]{1,0:T(4,128)S(1)}, u32[]{:S(2)}, u32[]{:S(2)}) collective-permute-start(f32[4,1024]{1,0:T(4,128)S(1)} %get-tuple-element.278), channel_id=1, source_target_pairs={{1,0},{2,1},{3,2},{4,3},{5,4},{6,5},{7,6},{8,7},{9,8},{10,9},{11,1... | collective-permute-start | bytes 49160 | tf_op jit(solution)/shard_map/while/body/eval_jaxpr/ppermute | solution.py:18
  81.2 6.6 %collective-permute-start.1 = (f32[4,1024]{1,0:T(4,128)S(1)}, f32[4,1024]{1,0:T(4,128)S(1)}, u32[]{:S(2)}, u32[]{:S(2)}) collective-permute-start(f32[4,1024]{1,0:T(4,128)S(1)} %get-tuple-element.279), channel_id=1, source_target_pairs={{0,1},{1,2},{2,3},{3,4},{4,5},{5,6},{6,7},{7,8},{8,9},{9,10},{10,1... | collective-permute-start | bytes 49160 | tf_op jit(solution)/shard_map/while/body/eval_jaxpr/ppermute | solution.py:17
  89.0 9.7 %copy-start.4 = (f32[32,1024]{1,0:T(8,128)S(1)}, f32[32,1024]{1,0:T(8,128)}, u32[]{:S(2)}) copy-start(f32[32,1024]{1,0:T(8,128)} %get-tuple-element.328) | copy-start | bytes 393220 | tf_op jit(solution)/shard_map/while
  89.0 8.6 %collective-permute-start = (f32[4,1024]{1,0:T(4,128)S(1)}, f32[4,1024]{1,0:T(4,128)S(1)}, u32[]{:S(2)}, u32[]{:S(2)}) collective-permute-start(f32[4,1024]{1,0:T(4,128)S(1)} %get-tuple-element.278), channel_id=1, source_target_pairs={{1,0},{2,1},{3,2},{4,3},{5,4},{6,5},{7,6},{8,7},{9,8},{10,9},{11,1... | collective-permute-start | bytes 49160 | tf_op jit(solution)/shard_map/while/body/eval_jaxpr/ppermute | solution.py:18
  91.1 6.6 %collective-permute-start.1 = (f32[4,1024]{1,0:T(4,128)S(1)}, f32[4,1024]{1,0:T(4,128)S(1)}, u32[]{:S(2)}, u32[]{:S(2)}) collective-permute-start(f32[4,1024]{1,0:T(4,128)S(1)} %get-tuple-element.279), channel_id=1, source_target_pairs={{0,1},{1,2},{2,3},{3,4},{4,5},{5,6},{6,7},{7,8},{8,9},{9,10},{10,1... | collective-permute-start | bytes 49160 | tf_op jit(solution)/shard_map/while/body/eval_jaxpr/ppermute | solution.py:17
  106.5 14.6 %copy-start.8 = (bf16[4,128]{1,0:T(4,128)(2,1)S(1)}, bf16[4,128]{1,0:T(4,128)(2,1)}, u32[]{:S(2)}) copy-start(bf16[4,128]{1,0:T(4,128)(2,1)} %param.17) | copy-start | bytes 3076
  106.5 71.7 %copy-start.7 = (bf16[128,512]{1,0:T(8,128)(2,1)S(1)}, bf16[128,512]{1,0:T(8,128)(2,1)}, u32[]{:S(2)}) copy-start(bf16[128,512]{1,0:T(8,128)(2,1)} %param.18) | copy-start | bytes 393220
  106.5 71.9 %copy-start.6 = (bf16[512,512]{1,0:T(8,128)(2,1)S(1)}, bf16[512,512]{1,0:T(8,128)(2,1)}, u32[]{:S(2)}) copy-start(bf16[512,512]{1,0:T(8,128)(2,1)} %param.19) | copy-start | bytes 1572868
  114.4 66.9 %all-to-all-start = ((bf16[8,2,32768]{2,1,0:T(2,128)(2,1)}), bf16[8,2,32768]{2,1,0:T(2,128)(2,1)S(1)}, u32[]{:S(2)}, u32[]{:S(2)}) async-start(bf16[8,2,32768]{2,1,0:T(2,128)(2,1)} %reshape.112), calls=%async_computation | async-start | bytes 2097152 | tf_op jit(solution)/shard_map/all_to_all | solution.py:118
  121.1 236.1 %all-reduce.10.cloned.1.call-start = ((), (), s32[]{:S(2)}) async-start(), calls=%async_computation.1 | async-start | bytes 2097152 | tf_op jit(solution)/shard_map/psum | solution.py:130
  178.9 1.0 copy-start.1
  197.4 8.9 %copy-start.9 = (bf16[512,32,128]{2,1,0:T(8,128)(2,1)S(1)}, bf16[512,32,128]{2,1,0:T(8,128)(2,1)}, u32[]{:S(2)}) copy-start(bf16[512,32,128]{2,1,0:T(8,128)(2,1)} %param.21) | copy-start | bytes 12582916
  204.3 2.0 copy-start.5
  206.3 3.9 %copy-start.3 = (f32[512,512]{1,0:T(8,128)S(1)}, f32[512,512]{1,0:T(8,128)}, u32[]{:S(2)}) copy-start(f32[512,512]{1,0:T(8,128)} %convolution_tanh_fusion) | copy-start | bytes 3145732
  214.8 144.2 %copy-start.2 = (f32[512,512]{1,0:T(8,128)S(1)}, f32[512,512]{1,0:T(8,128)}, u32[]{:S(2)}) copy-start(f32[512,512]{1,0:T(8,128)} %copy-done.1) | copy-start | bytes 3145732
Sparse Core Ops, SparseCore 0:
  210.3 146.8 all-reduce.9
where the time goes:
time: 376 us; the launch traced here: 374 us
  waiting for transfers between devices  140 us (37%)
  starting transfers between devices  59.1 us (16%)
  blocking collectives  57 us (15%)
  local copies, waits for them, and re-layouts  45.6 us (12%)
  matrix products  24.8 us (7%)
  loops' own time  22.1 us (6%)
  between operations  14.2 us (4%)
  other arithmetic  11.6 us (3%)
    psum x1, waiting for transfers between devices, per_device(): back_c = lax.psum(contract_cols(residual, weight_flat), ('group', 'strip'))  139 us
    all_gather x1, blocking collectives, per_device(): lax.all_gather(sample_inputs, ('group', 'strip'), axis=0, tiled=True)  57 us
    ppermute x9, starting transfers between devices, padded(): before = lax.ppermute(last, axis, up)  34 us
    another operation x1, loops' own time, per_device(): lax.fori_loop(0, STEPS // halo_width, block_steps, (field_now, start_hist...  22.1 us
    unnamed x24, local copies, waits for them, and re-layouts  22.1 us
    ppermute x9, starting transfers between devices, padded(): after = lax.ppermute(initial, axis, down)  18.3 us
    dot_general x4, matrix products, contract_rows(): lax.dot_general(left, right, (((0,), (0,)), ((), ())), preferred_element_...  10.6 us
  transfers between devices with their start and end apart: 20, of which 2 were waited for; matrix products, arithmetic and copies ran while one was open for 4% of the time, Pallas kernels for 0%

commit v1 on v0

--- a/solution.py
+++ b/solution.py
@@ -120,7 +120,12 @@
     targets = jnp.take(flat_snaps, assign, axis=0)
     weight_flat = w_out.reshape(w_out.shape[0], -1)
     inverse_root = 1.0 / jnp.sqrt(jnp.float32(assign.shape[0]))
-    all_inputs = lax.all_gather(sample_inputs, ("group", "strip"), axis=0, tiled=True)
+    all_inputs = jnp.concatenate(
+        lax.all_to_all(
+            jnp.stack([sample_inputs] * lax.axis_size(("group", "strip"))), ("group", "strip"), 0, 0
+        ),
+        axis=0,
+    )
     activations, hiddens = forward(all_inputs, w_first, w_second, w_third)
     hidden_all = hiddens[2]
     predicted = jnp.dot(hidden_all, weight_flat, preferred_element_type=jnp.float32)

time: 376 us -> 359 us (0.955)
  blocking collectives: 57 us -> 0 us
  waiting for transfers between devices: 140 us -> 168 us
  starting transfers between devices: 59.1 us -> 68.9 us
    all_gather x1 -> x0, blocking collectives: 57 us -> none  [per_device(): lax.all_gather(sample_inputs, ('group', 'strip'), axis=0, tiled=True)]
    psum x1, waiting for transfers between devices: 139 us -> 153 us  [per_device(): back_c = lax.psum(contract_cols(residual, weight_flat), ('group', 'strip'))]
    all_to_all x1, waiting for transfers between devices: 0.01 us -> 13.8 us  [per_device(): lax.all_to_all(snapshots[None], 'group', split_axis=3, concat_axis=0, til...]
    all_to_all x0 -> x1, starting transfers between devices: none -> 11.5 us  [per_device(): lax.all_to_all(jnp.stack([sample_inputs] * lax.axis_size(('group', 'strip...]
  transfers between devices with their start and end apart: 20 -> 21, of which waited for: 2 -> 3; matrix products, arithmetic and copies ran while one was open for 4% -> 12% of each run, Pallas kernels for 0% -> 0%
where the time goes in v1:
time: 359 us; the launch traced here: 357 us
  waiting for transfers between devices  168 us (47%)
  starting transfers between devices  68.9 us (19%)
  local copies, waits for them, and re-layouts  47 us (13%)
  matrix products  25.5 us (7%)
  loops' own time  22.1 us (6%)
  between operations  14.2 us (4%)
  other arithmetic  11.6 us (3%)
    psum x1, waiting for transfers between devices, per_device(): back_c = lax.psum(contract_cols(residual, weight_flat), ('group', 'strip'))  153 us
    ppermute x9, starting transfers between devices, padded(): before = lax.ppermute(last, axis, up)  32.8 us
    unnamed x24, local copies, waits for them, and re-layouts  22.2 us
    another operation x1, loops' own time, per_device(): lax.fori_loop(0, STEPS // halo_width, block_steps, (field_now, start_hist...  22.1 us
    ppermute x9, starting transfers between devices, padded(): after = lax.ppermute(initial, axis, down)  18.3 us
    all_to_all x1, waiting for transfers between devices, per_device(): lax.all_to_all(snapshots[None], 'group', split_axis=3, concat_axis=0, til...  13.8 us
    all_to_all x1, starting transfers between devices, per_device(): lax.all_to_all(jnp.stack([sample_inputs] * lax.axis_size(('group', 'strip...  11.5 us
    dot_general x4, matrix products, contract_rows(): lax.dot_general(left, right, (((0,), (0,)), ((), ())), preferred_element_...  11.3 us
  transfers between devices with their start and end apart: 21, of which 3 were waited for; matrix products, arithmetic and copies ran while one was open for 12% of the time, Pallas kernels for 0%

profile of v1, /device:TPU:1, one launch (start us, length us, event | category | flops | bytes accessed | tf_op | source)
XLA Modules:
  0.0 357.0 jit_solution(7118428843459678485)
XLA Ops:
  7.2 1.0 copy.49
  8.1 1.4 stack.2
  9.5 11.5 %all-to-all-start = ((bf16[128,4,128]{2,1,0:T(4,128)(2,1)}), bf16[128,4,128]{2,1,0:T(4,128)(2,1)S(1)}, u32[]{:S(2)}, u32[]{:S(2)}) async-start(bf16[128,4,128]{2,1,0:T(4,128)(2,1)} %stack.2), calls=%async_computation | async-start | bytes 262144 | tf_op jit(solution)/shard_map/all_to_all | solution.py:124
  21.0 0.8 slice_bitcast_fusion.5
  21.8 3.6 %collective-permute-start.2 = (f32[4,1024]{1,0:T(4,128)S(1)}, f32[4,1024]{1,0:T(4,128)S(1)}, u32[]{:S(2)}, u32[]{:S(2)}) collective-permute-start(f32[4,1024]{1,0:T(4,128)S(1)} %get-tuple-element.221), channel_id=1, source_target_pairs={{0,1},{1,2},{2,3},{3,4},{4,5},{5,6},{6,7},{7,8},{8,9},{9,10},{10,1... | collective-permute-start | bytes 49160 | tf_op jit(solution)/shard_map/ppermute | solution.py:17
  25.4 1.9 collective-permute-start.3
  27.4 0.7 fusion.55
  28.0 0.7 compare_and_fusion
  28.7 0.7 compare_select_fusion
  29.4 0.7 compare_and_fusion.1
  30.1 0.7 collective-permute-done.3
  30.8 0.9 pad_maximum_fusion.1
  31.7 0.3 broadcast_in_dim.69
  32.0 78.7 %while.17 = (s32[]{:T(128)}, f32[32,1024]{1,0:T(8,128)S(1)}, bf16[32,32,1024]{2,1,0:T(8,128)(2,1)S(1)}, s32[]{:T(128)}, f32[40,1024]{1,0:T(8,128)S(1)}, /*index=...) while((s32[]{:T(128)}, f32[32,1024]{1,0:T(8,128)S(1)}, ...), condition=%wide.region_1.2_spmd, body=%wide.region_0.1_spmd.sunk | while | flops 1978390 | bytes 7814625 | solution.py:114
  32.0 2.1 collective-permute-start
  34.1 3.6 %collective-permute-start.1 = (f32[4,1024]{1,0:T(4,128)S(1)}, f32[4,1024]{1,0:T(4,128)S(1)}, u32[]{:S(2)}, u32[]{:S(2)}) collective-permute-start(f32[4,1024]{1,0:T(4,128)S(1)} %get-tuple-element.279), channel_id=1, source_target_pairs={{0,1},{1,2},{2,3},{3,4},{4,5},{5,6},{6,7},{7,8},{8,9},{9,10},{10,1... | collective-permute-start | bytes 49160 | tf_op jit(solution)/shard_map/while/body/eval_jaxpr/ppermute | solution.py:17
  40.8 0.1 fusion.89
  41.9 2.1 collective-permute-start
  43.9 3.6 %collective-permute-start.1 = (f32[4,1024]{1,0:T(4,128)S(1)}, f32[4,1024]{1,0:T(4,128)S(1)}, u32[]{:S(2)}, u32[]{:S(2)}) collective-permute-start(f32[4,1024]{1,0:T(4,128)S(1)} %get-tuple-element.279), channel_id=1, source_target_pairs={{0,1},{1,2},{2,3},{3,4},{4,5},{5,6},{6,7},{7,8},{8,9},{9,10},{10,1... | collective-permute-start | bytes 49160 | tf_op jit(solution)/shard_map/while/body/eval_jaxpr/ppermute | solution.py:17
  50.7 0.1 fusion.89
  50.9 0.1 fusion.92
  51.7 2.1 collective-permute-start
  53.8 3.6 %collective-permute-start.1 = (f32[4,1024]{1,0:T(4,128)S(1)}, f32[4,1024]{1,0:T(4,128)S(1)}, u32[]{:S(2)}, u32[]{:S(2)}) collective-permute-start(f32[4,1024]{1,0:T(4,128)S(1)} %get-tuple-element.279), channel_id=1, source_target_pairs={{0,1},{1,2},{2,3},{3,4},{4,5},{5,6},{6,7},{7,8},{8,9},{9,10},{10,1... | collective-permute-start | bytes 49160 | tf_op jit(solution)/shard_map/while/body/eval_jaxpr/ppermute | solution.py:17
  60.5 0.1 fusion.89
  60.8 0.1 fusion.92
  61.6 2.1 collective-permute-start
  63.6 3.6 %collective-permute-start.1 = (f32[4,1024]{1,0:T(4,128)S(1)}, f32[4,1024]{1,0:T(4,128)S(1)}, u32[]{:S(2)}, u32[]{:S(2)}) collective-permute-start(f32[4,1024]{1,0:T(4,128)S(1)} %get-tuple-element.279), channel_id=1, source_target_pairs={{0,1},{1,2},{2,3},{3,4},{4,5},{5,6},{6,7},{7,8},{8,9},{9,10},{10,1... | collective-permute-start | bytes 49160 | tf_op jit(solution)/shard_map/while/body/eval_jaxpr/ppermute | solution.py:17
  70.3 0.1 fusion.89
  70.6 0.1 fusion.92
  71.4 2.1 collective-permute-start
  73.5 3.6 %collective-permute-start.1 = (f32[4,1024]{1,0:T(4,128)S(1)}, f32[4,1024]{1,0:T(4,128)S(1)}, u32[]{:S(2)}, u32[]{:S(2)}) collective-permute-start(f32[4,1024]{1,0:T(4,128)S(1)} %get-tuple-element.279), channel_id=1, source_target_pairs={{0,1},{1,2},{2,3},{3,4},{4,5},{5,6},{6,7},{7,8},{8,9},{9,10},{10,1... | collective-permute-start | bytes 49160 | tf_op jit(solution)/shard_map/while/body/eval_jaxpr/ppermute | solution.py:17
  80.2 0.1 fusion.89
  81.2 2.1 collective-permute-start
  83.3 3.6 %collective-permute-start.1 = (f32[4,1024]{1,0:T(4,128)S(1)}, f32[4,1024]{1,0:T(4,128)S(1)}, u32[]{:S(2)}, u32[]{:S(2)}) collective-permute-start(f32[4,1024]{1,0:T(4,128)S(1)} %get-tuple-element.279), channel_id=1, source_target_pairs={{0,1},{1,2},{2,3},{3,4},{4,5},{5,6},{6,7},{7,8},{8,9},{9,10},{10,1... | collective-permute-start | bytes 49160 | tf_op jit(solution)/shard_map/while/body/eval_jaxpr/ppermute | solution.py:17
  91.1 2.1 collective-permute-start
  93.1 3.6 %collective-permute-start.1 = (f32[4,1024]{1,0:T(4,128)S(1)}, f32[4,1024]{1,0:T(4,128)S(1)}, u32[]{:S(2)}, u32[]{:S(2)}) collective-permute-start(f32[4,1024]{1,0:T(4,128)S(1)} %get-tuple-element.279), channel_id=1, source_target_pairs={{0,1},{1,2},{2,3},{3,4},{4,5},{5,6},{6,7},{7,8},{8,9},{9,10},{10,1... | collective-permute-start | bytes 49160 | tf_op jit(solution)/shard_map/while/body/eval_jaxpr/ppermute | solution.py:17
  100.9 2.1 collective-permute-start
  103.0 3.6 %collective-permute-start.1 = (f32[4,1024]{1,0:T(4,128)S(1)}, f32[4,1024]{1,0:T(4,128)S(1)}, u32[]{:S(2)}, u32[]{:S(2)}) collective-permute-start(f32[4,1024]{1,0:T(4,128)S(1)} %get-tuple-element.279), channel_id=1, source_target_pairs={{0,1},{1,2},{2,3},{3,4},{4,5},{5,6},{6,7},{7,8},{8,9},{9,10},{10,1... | collective-permute-start | bytes 49160 | tf_op jit(solution)/shard_map/while/body/eval_jaxpr/ppermute | solution.py:17
  110.7 1.6 gather_fusion
  112.3 1.4 bitcast_select_fusion
  113.7 4.7 %copy.18 = bf16[1,16,32,1024]{2,1,0,3:T(8,128)(2,1)} copy(bf16[1,16,32,1024]{3,2,1,0:T(8,128)(2,1)S(1)} %bitcast_select_fusion) | data formatting | bytes 2097152 | tf_op jit(solution)/shard_map/jit(_take)/select_n | solution.py:117
  118.4 7.9 %reshape.116 = bf16[8,2,32768]{2,1,0:T(2,128)(2,1)} reshape(bf16[1024,1,16,32]{3,2,1,0:T(8,128)(2,1)} %bitcast.93) | data formatting | bytes 2097152
  126.3 6.2 %all-to-all-start.1 = ((bf16[8,2,32768]{2,1,0:T(2,128)(2,1)}), bf16[8,2,32768]{2,1,0:T(2,128)(2,1)S(1)}, u32[]{:S(2)}, u32[]{:S(2)}) async-start(bf16[8,2,32768]{2,1,0:T(2,128)(2,1)} %reshape.116), calls=%async_computation.1 | async-start | bytes 2097152 | tf_op jit(solution)/shard_map/all_to_all | solution.py:118
  132.6 0.3 convolution_tanh_fusion.2
  132.9 0.4 convolution_tanh_fusion.1
  133.4 1.0 copy-done.1
  134.4 1.4 convolution_tanh_fusion
  135.8 13.8 %all-to-all-done.1 = bf16[8,2,32768]{2,1,0:T(2,128)(2,1)S(1)} async-done(((bf16[8,2,32768]{2,1,0:T(2,128)(2,1)}), bf16[8,2,32768]{2,1,0:T(2,128)(2,1)S(1)}, u32[]{:S(2)}, u32[]{:S(2)}) %all-to-all-start.1) | async-done | bytes 1048608 | tf_op jit(solution)/shard_map/all_to_all | solution.py:118
  149.6 4.5 %reshape.117 = bf16[1024,1,16,32]{3,2,1,0:T(8,128)(2,1)} reshape(bf16[8,2,32768]{2,1,0:T(2,128)(2,1)S(1)} %all-to-all-done.1) | data formatting | bytes 2097152
  154.0 5.5 %copy.19 = bf16[1,16,32,8,128]{4,2,1,3,0:T(8,128)(2,1)} copy(bf16[1,16,32,8,128]{2,1,4,3,0:T(8,128)(2,1)} %bitcast.94) | data formatting | bytes 2097152 | tf_op jit(solution)/shard_map/all_to_all | solution.py:118
  159.6 1.7 copy.33
  161.3 4.4 %gather_fusion.1 = bf16[512,4096]{1,0:T(8,128)(2,1)} fusion(bf16[128,4096]{1,0:T(8,128)(2,1)S(1)} %bitcast.92, s32[1024]{0:T(1024)S(1)} %pad_clamp_fusion), kind=kCustom, calls=%fused_computation.1 | custom fusion | bytes 8390656 | tf_op jit(solution)/shard_map/jit(_take)/gather | solution.py:120
  165.6 6.9 %multiply_convert_fusion = bf16[512,4096]{1,0:T(8,128)(2,1)S(1)} fusion(bf16[512,4096]{1,0:T(8,128)(2,1)} %gather_fusion.1, pred[512]{0:T(512)(128)(4,1)S(1)} %compare_and_fusion.1, bf16[64,8,32,128]{3,2,1,0:T(8,128)(2,1)} %bitcast.102, f32[512,512]{1,0:T(8,128)} %convolution_tanh_fusion), kind=kOutput, calls=%fused_computation.49 | convolution fusion | flops 2158231552 | bytes 13632000 | tf_op jit(solution)/shard_map/dot_general | solution.py:131
  172.5 2.0 copy-done.5
  174.5 3.9 %fusion.34 = f32[512,512]{1,0:T(8,128)} fusion(bf16[512,4096]{1,0:T(8,128)(2,1)S(1)} %multiply_convert_fusion, bf16[64,8,32,128]{3,2,1,0:T(8,128)(2,1)S(1)} %bitcast.103), kind=kOutput, calls=%fused_computation.51 | convolution fusion | flops 2147483648 | bytes 9437184 | tf_op jit(solution)/shard_map/dot_general | solution.py:45
  178.5 4.6 %fusion.39 = bf16[64,8,32,128]{3,1,2,0:T(8,128)(2,1)S(1)} fusion(bf16[512,4096]{1,0:T(8,128)(2,1)} %copy-done.5, f32[512,512]{1,0:T(8,128)S(1)} %copy-done.3), kind=kOutput, calls=%fused_computation.56 | convolution fusion | flops 2149842944 | bytes 9437184 | tf_op jit(solution)/shard_map/dot_general | solution.py:39
  183.1 3.3 copy.23
  186.3 153.1 %all-reduce.10.cloned.1.call-done = f32[512,512]{1,0:T(8,128)} async-done(((f32[512,512]{1,0:T(8,128)}), f32[512,512]{1,0:T(8,128)}) %all-reduce.10.cloned.1.call-update) | async-done | bytes 1048592 | tf_op jit(solution)/shard_map/psum | solution.py:135
  339.5 1.8 multiply_convert_fusion.1
  341.3 1.3 fusion.40
  342.6 2.8 fusion.43
  345.4 2.5 fusion.52
  347.9 1.4 fusion.49
  349.3 0.8 copy.20
  (183 shorter events, 10.0 us)
Async XLA Ops:
  7.2 127.2 %copy-start = (bf16[512,512]{1,0:T(8,128)(2,1)S(1)}, bf16[512,512]{1,0:T(8,128)(2,1)}, u32[]{:S(2)}) copy-start(bf16[512,512]{1,0:T(8,128)(2,1)} %param.20) | copy-start | bytes 1572868
  9.5 116.8 %all-to-all-start = ((bf16[128,4,128]{2,1,0:T(4,128)(2,1)}), bf16[128,4,128]{2,1,0:T(4,128)(2,1)S(1)}, u32[]{:S(2)}, u32[]{:S(2)}) async-start(bf16[128,4,128]{2,1,0:T(4,128)(2,1)} %stack.2), calls=%async_computation | async-start | bytes 262144 | tf_op jit(solution)/shard_map/all_to_all | solution.py:124
  21.8 8.3 %collective-permute-start.2 = (f32[4,1024]{1,0:T(4,128)S(1)}, f32[4,1024]{1,0:T(4,128)S(1)}, u32[]{:S(2)}, u32[]{:S(2)}) collective-permute-start(f32[4,1024]{1,0:T(4,128)S(1)} %get-tuple-element.221), channel_id=1, source_target_pairs={{0,1},{1,2},{2,3},{3,4},{4,5},{5,6},{6,7},{7,8},{8,9},{9,10},{10,1... | collective-permute-start | bytes 49160 | tf_op jit(solution)/shard_map/ppermute | solution.py:17
  25.4 5.4 %collective-permute-start.3 = (f32[4,1024]{1,0:T(4,128)S(1)}, f32[4,1024]{1,0:T(4,128)S(1)}, u32[]{:S(2)}, u32[]{:S(2)}) collective-permute-start(f32[4,1024]{1,0:T(4,128)S(1)} %get-tuple-element.222), channel_id=1, source_target_pairs={{1,0},{2,1},{3,2},{4,3},{5,4},{6,5},{7,6},{8,7},{9,8},{10,9},{11,1... | collective-permute-start | bytes 49160 | tf_op jit(solution)/shard_map/ppermute | solution.py:18
  32.0 9.7 %copy-start.4 = (f32[32,1024]{1,0:T(8,128)S(1)}, f32[32,1024]{1,0:T(8,128)}, u32[]{:S(2)}) copy-start(f32[32,1024]{1,0:T(8,128)} %get-tuple-element.328) | copy-start | bytes 393220 | tf_op jit(solution)/shard_map/while
  32.0 8.6 %collective-permute-start = (f32[4,1024]{1,0:T(4,128)S(1)}, f32[4,1024]{1,0:T(4,128)S(1)}, u32[]{:S(2)}, u32[]{:S(2)}) collective-permute-start(f32[4,1024]{1,0:T(4,128)S(1)} %get-tuple-element.278), channel_id=1, source_target_pairs={{1,0},{2,1},{3,2},{4,3},{5,4},{6,5},{7,6},{8,7},{9,8},{10,9},{11,1... | collective-permute-start | bytes 49160 | tf_op jit(solution)/shard_map/while/body/eval_jaxpr/ppermute | solution.py:18
  34.1 6.6 %collective-permute-start.1 = (f32[4,1024]{1,0:T(4,128)S(1)}, f32[4,1024]{1,0:T(4,128)S(1)}, u32[]{:S(2)}, u32[]{:S(2)}) collective-permute-start(f32[4,1024]{1,0:T(4,128)S(1)} %get-tuple-element.279), channel_id=1, source_target_pairs={{0,1},{1,2},{2,3},{3,4},{4,5},{5,6},{6,7},{7,8},{8,9},{9,10},{10,1... | collective-permute-start | bytes 49160 | tf_op jit(solution)/shard_map/while/body/eval_jaxpr/ppermute | solution.py:17
  41.8 9.7 %copy-start.4 = (f32[32,1024]{1,0:T(8,128)S(1)}, f32[32,1024]{1,0:T(8,128)}, u32[]{:S(2)}) copy-start(f32[32,1024]{1,0:T(8,128)} %get-tuple-element.328) | copy-start | bytes 393220 | tf_op jit(solution)/shard_map/while
  41.9 8.6 %collective-permute-start = (f32[4,1024]{1,0:T(4,128)S(1)}, f32[4,1024]{1,0:T(4,128)S(1)}, u32[]{:S(2)}, u32[]{:S(2)}) collective-permute-start(f32[4,1024]{1,0:T(4,128)S(1)} %get-tuple-element.278), channel_id=1, source_target_pairs={{1,0},{2,1},{3,2},{4,3},{5,4},{6,5},{7,6},{8,7},{9,8},{10,9},{11,1... | collective-permute-start | bytes 49160 | tf_op jit(solution)/shard_map/while/body/eval_jaxpr/ppermute | solution.py:18
  43.9 6.6 %collective-permute-start.1 = (f32[4,1024]{1,0:T(4,128)S(1)}, f32[4,1024]{1,0:T(4,128)S(1)}, u32[]{:S(2)}, u32[]{:S(2)}) collective-permute-start(f32[4,1024]{1,0:T(4,128)S(1)} %get-tuple-element.279), channel_id=1, source_target_pairs={{0,1},{1,2},{2,3},{3,4},{4,5},{5,6},{6,7},{7,8},{8,9},{9,10},{10,1... | collective-permute-start | bytes 49160 | tf_op jit(solution)/shard_map/while/body/eval_jaxpr/ppermute | solution.py:17
  51.7 9.7 %copy-start.4 = (f32[32,1024]{1,0:T(8,128)S(1)}, f32[32,1024]{1,0:T(8,128)}, u32[]{:S(2)}) copy-start(f32[32,1024]{1,0:T(8,128)} %get-tuple-element.328) | copy-start | bytes 393220 | tf_op jit(solution)/shard_map/while
  51.7 8.6 %collective-permute-start = (f32[4,1024]{1,0:T(4,128)S(1)}, f32[4,1024]{1,0:T(4,128)S(1)}, u32[]{:S(2)}, u32[]{:S(2)}) collective-permute-start(f32[4,1024]{1,0:T(4,128)S(1)} %get-tuple-element.278), channel_id=1, source_target_pairs={{1,0},{2,1},{3,2},{4,3},{5,4},{6,5},{7,6},{8,7},{9,8},{10,9},{11,1... | collective-permute-start | bytes 49160 | tf_op jit(solution)/shard_map/while/body/eval_jaxpr/ppermute | solution.py:18
  53.8 6.6 %collective-permute-start.1 = (f32[4,1024]{1,0:T(4,128)S(1)}, f32[4,1024]{1,0:T(4,128)S(1)}, u32[]{:S(2)}, u32[]{:S(2)}) collective-permute-start(f32[4,1024]{1,0:T(4,128)S(1)} %get-tuple-element.279), channel_id=1, source_target_pairs={{0,1},{1,2},{2,3},{3,4},{4,5},{5,6},{6,7},{7,8},{8,9},{9,10},{10,1... | collective-permute-start | bytes 49160 | tf_op jit(solution)/shard_map/while/body/eval_jaxpr/ppermute | solution.py:17
  61.5 9.7 %copy-start.4 = (f32[32,1024]{1,0:T(8,128)S(1)}, f32[32,1024]{1,0:T(8,128)}, u32[]{:S(2)}) copy-start(f32[32,1024]{1,0:T(8,128)} %get-tuple-element.328) | copy-start | bytes 393220 | tf_op jit(solution)/shard_map/while
  61.6 8.6 %collective-permute-start = (f32[4,1024]{1,0:T(4,128)S(1)}, f32[4,1024]{1,0:T(4,128)S(1)}, u32[]{:S(2)}, u32[]{:S(2)}) collective-permute-start(f32[4,1024]{1,0:T(4,128)S(1)} %get-tuple-element.278), channel_id=1, source_target_pairs={{1,0},{2,1},{3,2},{4,3},{5,4},{6,5},{7,6},{8,7},{9,8},{10,9},{11,1... | collective-permute-start | bytes 49160 | tf_op jit(solution)/shard_map/while/body/eval_jaxpr/ppermute | solution.py:18
  63.6 6.6 %collective-permute-start.1 = (f32[4,1024]{1,0:T(4,128)S(1)}, f32[4,1024]{1,0:T(4,128)S(1)}, u32[]{:S(2)}, u32[]{:S(2)}) collective-permute-start(f32[4,1024]{1,0:T(4,128)S(1)} %get-tuple-element.279), channel_id=1, source_target_pairs={{0,1},{1,2},{2,3},{3,4},{4,5},{5,6},{6,7},{7,8},{8,9},{9,10},{10,1... | collective-permute-start | bytes 49160 | tf_op jit(solution)/shard_map/while/body/eval_jaxpr/ppermute | solution.py:17
  71.4 9.7 %copy-start.4 = (f32[32,1024]{1,0:T(8,128)S(1)}, f32[32,1024]{1,0:T(8,128)}, u32[]{:S(2)}) copy-start(f32[32,1024]{1,0:T(8,128)} %get-tuple-element.328) | copy-start | bytes 393220 | tf_op jit(solution)/shard_map/while
  71.4 8.6 %collective-permute-start = (f32[4,1024]{1,0:T(4,128)S(1)}, f32[4,1024]{1,0:T(4,128)S(1)}, u32[]{:S(2)}, u32[]{:S(2)}) collective-permute-start(f32[4,1024]{1,0:T(4,128)S(1)} %get-tuple-element.278), channel_id=1, source_target_pairs={{1,0},{2,1},{3,2},{4,3},{5,4},{6,5},{7,6},{8,7},{9,8},{10,9},{11,1... | collective-permute-start | bytes 49160 | tf_op jit(solution)/shard_map/while/body/eval_jaxpr/ppermute | solution.py:18
  73.5 6.6 %collective-permute-start.1 = (f32[4,1024]{1,0:T(4,128)S(1)}, f32[4,1024]{1,0:T(4,128)S(1)}, u32[]{:S(2)}, u32[]{:S(2)}) collective-permute-start(f32[4,1024]{1,0:T(4,128)S(1)} %get-tuple-element.279), channel_id=1, source_target_pairs={{0,1},{1,2},{2,3},{3,4},{4,5},{5,6},{6,7},{7,8},{8,9},{9,10},{10,1... | collective-permute-start | bytes 49160 | tf_op jit(solution)/shard_map/while/body/eval_jaxpr/ppermute | solution.py:17
  81.2 9.7 %copy-start.4 = (f32[32,1024]{1,0:T(8,128)S(1)}, f32[32,1024]{1,0:T(8,128)}, u32[]{:S(2)}) copy-start(f32[32,1024]{1,0:T(8,128)} %get-tuple-element.328) | copy-start | bytes 393220 | tf_op jit(solution)/shard_map/while
  81.2 8.6 %collective-permute-start = (f32[4,1024]{1,0:T(4,128)S(1)}, f32[4,1024]{1,0:T(4,128)S(1)}, u32[]{:S(2)}, u32[]{:S(2)}) collective-permute-start(f32[4,1024]{1,0:T(4,128)S(1)} %get-tuple-element.278), channel_id=1, source_target_pairs={{1,0},{2,1},{3,2},{4,3},{5,4},{6,5},{7,6},{8,7},{9,8},{10,9},{11,1... | collective-permute-start | bytes 49160 | tf_op jit(solution)/shard_map/while/body/eval_jaxpr/ppermute | solution.py:18
  83.3 6.6 %collective-permute-start.1 = (f32[4,1024]{1,0:T(4,128)S(1)}, f32[4,1024]{1,0:T(4,128)S(1)}, u32[]{:S(2)}, u32[]{:S(2)}) collective-permute-start(f32[4,1024]{1,0:T(4,128)S(1)} %get-tuple-element.279), channel_id=1, source_target_pairs={{0,1},{1,2},{2,3},{3,4},{4,5},{5,6},{6,7},{7,8},{8,9},{9,10},{10,1... | collective-permute-start | bytes 49160 | tf_op jit(solution)/shard_map/while/body/eval_jaxpr/ppermute | solution.py:17
  91.0 9.7 %copy-start.4 = (f32[32,1024]{1,0:T(8,128)S(1)}, f32[32,1024]{1,0:T(8,128)}, u32[]{:S(2)}) copy-start(f32[32,1024]{1,0:T(8,128)} %get-tuple-element.328) | copy-start | bytes 393220 | tf_op jit(solution)/shard_map/while
  91.1 8.6 %collective-permute-start = (f32[4,1024]{1,0:T(4,128)S(1)}, f32[4,1024]{1,0:T(4,128)S(1)}, u32[]{:S(2)}, u32[]{:S(2)}) collective-permute-start(f32[4,1024]{1,0:T(4,128)S(1)} %get-tuple-element.278), channel_id=1, source_target_pairs={{1,0},{2,1},{3,2},{4,3},{5,4},{6,5},{7,6},{8,7},{9,8},{10,9},{11,1... | collective-permute-start | bytes 49160 | tf_op jit(solution)/shard_map/while/body/eval_jaxpr/ppermute | solution.py:18
  93.1 6.6 %collective-permute-start.1 = (f32[4,1024]{1,0:T(4,128)S(1)}, f32[4,1024]{1,0:T(4,128)S(1)}, u32[]{:S(2)}, u32[]{:S(2)}) collective-permute-start(f32[4,1024]{1,0:T(4,128)S(1)} %get-tuple-element.279), channel_id=1, source_target_pairs={{0,1},{1,2},{2,3},{3,4},{4,5},{5,6},{6,7},{7,8},{8,9},{9,10},{10,1... | collective-permute-start | bytes 49160 | tf_op jit(solution)/shard_map/while/body/eval_jaxpr/ppermute | solution.py:17
  100.9 9.7 %copy-start.4 = (f32[32,1024]{1,0:T(8,128)S(1)}, f32[32,1024]{1,0:T(8,128)}, u32[]{:S(2)}) copy-start(f32[32,1024]{1,0:T(8,128)} %get-tuple-element.328) | copy-start | bytes 393220 | tf_op jit(solution)/shard_map/while
  100.9 8.6 %collective-permute-start = (f32[4,1024]{1,0:T(4,128)S(1)}, f32[4,1024]{1,0:T(4,128)S(1)}, u32[]{:S(2)}, u32[]{:S(2)}) collective-permute-start(f32[4,1024]{1,0:T(4,128)S(1)} %get-tuple-element.278), channel_id=1, source_target_pairs={{1,0},{2,1},{3,2},{4,3},{5,4},{6,5},{7,6},{8,7},{9,8},{10,9},{11,1... | collective-permute-start | bytes 49160 | tf_op jit(solution)/shard_map/while/body/eval_jaxpr/ppermute | solution.py:18
  103.0 6.6 %collective-permute-start.1 = (f32[4,1024]{1,0:T(4,128)S(1)}, f32[4,1024]{1,0:T(4,128)S(1)}, u32[]{:S(2)}, u32[]{:S(2)}) collective-permute-start(f32[4,1024]{1,0:T(4,128)S(1)} %get-tuple-element.279), channel_id=1, source_target_pairs={{0,1},{1,2},{2,3},{3,4},{4,5},{5,6},{6,7},{7,8},{8,9},{9,10},{10,1... | collective-permute-start | bytes 49160 | tf_op jit(solution)/shard_map/while/body/eval_jaxpr/ppermute | solution.py:17
  118.4 14.2 %copy-start.8 = (bf16[128,512]{1,0:T(8,128)(2,1)S(1)}, bf16[128,512]{1,0:T(8,128)(2,1)}, u32[]{:S(2)}) copy-start(bf16[128,512]{1,0:T(8,128)(2,1)} %param.18) | copy-start | bytes 393220
  118.4 14.5 %copy-start.6 = (bf16[512,512]{1,0:T(8,128)(2,1)S(1)}, bf16[512,512]{1,0:T(8,128)(2,1)}, u32[]{:S(2)}) copy-start(bf16[512,512]{1,0:T(8,128)(2,1)} %param.19) | copy-start | bytes 1572868
  126.3 23.3 %all-to-all-start.1 = ((bf16[8,2,32768]{2,1,0:T(2,128)(2,1)}), bf16[8,2,32768]{2,1,0:T(2,128)(2,1)S(1)}, u32[]{:S(2)}, u32[]{:S(2)}) async-start(bf16[8,2,32768]{2,1,0:T(2,128)(2,1)} %reshape.116), calls=%async_computation.1 | async-start | bytes 2097152 | tf_op jit(solution)/shard_map/all_to_all | solution.py:118
  132.6 206.9 %all-reduce.10.cloned.1.call-start = ((), (), s32[]{:S(2)}) async-start(), calls=%async_computation.2 | async-start | bytes 2097152 | tf_op jit(solution)/shard_map/psum | solution.py:135
  133.4 1.0 copy-start.1
  165.6 8.9 %copy-start.9 = (bf16[512,32,128]{2,1,0:T(8,128)(2,1)S(1)}, bf16[512,32,128]{2,1,0:T(8,128)(2,1)}, u32[]{:S(2)}) copy-start(bf16[512,32,128]{2,1,0:T(8,128)(2,1)} %param.21) | copy-start | bytes 12582916
  172.5 2.0 copy-start.5
  174.5 3.9 %copy-start.3 = (f32[512,512]{1,0:T(8,128)S(1)}, f32[512,512]{1,0:T(8,128)}, u32[]{:S(2)}) copy-start(f32[512,512]{1,0:T(8,128)} %convolution_tanh_fusion) | copy-start | bytes 3145732
  183.1 158.2 %copy-start.2 = (f32[512,512]{1,0:T(8,128)S(1)}, f32[512,512]{1,0:T(8,128)}, u32[]{:S(2)}) copy-start(f32[512,512]{1,0:T(8,128)} %copy-done.1) | copy-start | bytes 3145732
  345.4 4.0 %copy-start.7 = (f32[128,512]{0,1:T(8,128)S(1)}, f32[128,512]{0,1:T(8,128)}, u32[]{:S(2)}) copy-start(f32[128,512]{0,1:T(8,128)} %fusion.43) | copy-start | bytes 786436
Sparse Core Ops, SparseCore 0:
  178.6 160.8 all-reduce.9
